TPU v7x, 128 devices: a whole 4x4x4 slice. The times are simulated.
128 devices in a mesh: row: 16 (over y, z), col: 8 (over x, core).
Axes of the slice: x: 4, y: 4, z: 4, core: 2. Of those that a mesh axis runs over, the one named last changes fastest.
Arguments:
- child_parent: int32 [16384], P(('row', 'col')), may hold values from 0 to 4095, as said below
- prefix_len: int32 [16384], P(('row', 'col')), may hold values from 1 to 40
- child_delta: bfloat16 [16384, 3584], P(('row', 'col')), may hold values from -6 to 6
- parent_hidden: bfloat16 [4096, 3584], P(('row', 'col')), may hold values from -6 to 6
- parent_cache: bfloat16 [4096, 2, 2, 128, 128], P(('row', 'col')), may hold values from -720 to 720
- prefix_cache: bfloat16 [128, 2, 2, 5120, 128], P(('row', 'col')), may hold values from -720 to 720
- norm_gain: float32 [3584], replicated, may hold values from 0.1 to 1.9
- w_query: bfloat16 [3584, 1792], replicated, may hold values from -0.09375 to 0.09375
- w_kv: bfloat16 [3584, 512], replicated, may hold values from -0.09375 to 0.09375
Outputs:
- context: bfloat16 [16384, 1792], P(('row', 'col'))
- child_kv: bfloat16 [16384, 512], P(('row', 'col'))
Inputs may be any that keep to these rules, and one draw needn't show every extreme that they name: `child_parent`: each device's 128 children name exactly 16 parents held in each column of devices; the children of any one row of devices name exactly 8 parents held by any one device; one device's children name at most 2 parents held by one device, and exactly 2 for some pairs. Parent p is held by device p // 32, device index = row index * 8 + column index.
All inputs are finite; a program needn't handle non-finite values.
Results may differ from a plain program's by a relative error of at most 0.0085.
The roundings to bfloat16 on the way count: a program that leaves them out, or rounds other values in their place, can miss the bound.
Values may be sent and summed in bfloat16 or wider, within the bound.
A program may use at most 256 MiB of HBM per device.

v0:
```python
import math
import jax
import jax.numpy as jnp
from jax import lax
from jax.sharding import PartitionSpec as P

EPSILON = 1e-06


def side_by_side(arrays, axis, split_dim, concat_dim, along):
    widths = [a.shape[along] for a in arrays]
    both = jnp.concatenate(arrays, axis=along)
    result = lax.all_to_all(both, axis, split_axis=split_dim, concat_axis=concat_dim, tiled=True)
    return tuple(jnp.split(result, [sum(widths[:k]) for k in range(1, len(widths))], axis=along))


def project_rows(parent_rows, delta_rows, norm_gain, w_query, w_kv):
    widened = parent_rows.astype(jnp.float32) + delta_rows.astype(jnp.float32)
    inverse = lax.rsqrt(jnp.mean(widened * widened, axis=-1, keepdims=True) + EPSILON)
    normed = (widened * inverse * norm_gain).astype(jnp.bfloat16)
    queries = jnp.dot(normed, w_query, preferred_element_type=jnp.float32).astype(jnp.bfloat16)
    new_kv = jnp.dot(normed, w_kv, preferred_element_type=jnp.float32).astype(jnp.bfloat16)
    return (queries, new_kv)


def prefix_scores(grouped, block_counts, prefix_rows, block_tokens, scale_factor):
    score_pre = (
        jnp.einsum("chgd,hld->hcgl", grouped, prefix_rows[0], preferred_element_type=jnp.float32)
        * scale_factor
    )
    key_positions = jnp.arange(prefix_rows.shape[2], dtype=jnp.int32)
    limits = block_counts * block_tokens
    in_prefix = key_positions[None, None, None, :] < limits[None, :, None, None]
    return jnp.where(in_prefix, score_pre, -jnp.inf)


def pick_slots(member, rank_grid, values, slot_count):
    wanted = jnp.arange(slot_count, dtype=jnp.int32)
    match_mask = member[..., None, :] & (rank_grid[..., None, :] == wanted[:, None])
    return jnp.sum(jnp.where(match_mask, values[..., None, :], 0), axis=-1)


def direct_layout(
    whole_source, whole_local, my_source, my_device, device_count, per_device, capacity
):
    positions = jnp.arange(per_device, dtype=jnp.int32)
    source_grid = whole_source.reshape(device_count, per_device)
    local_grid = whole_local.reshape(device_count, per_device)
    member = source_grid == my_device
    rank_grid = jnp.cumsum(member.astype(jnp.int32), axis=1) - 1
    send_ids = pick_slots(member, rank_grid, local_grid, capacity)
    earlier = (my_source[None, :] == my_source[:, None]) & (positions[None, :] < positions[:, None])
    my_rank = jnp.sum(earlier.astype(jnp.int32), axis=1)
    return (send_ids, my_source * capacity + my_rank)


def heads_to_rows(stat, child_count):
    return jnp.transpose(stat[..., 0], (1, 0, 2)).reshape(child_count, -1)


def rows_to_heads(stat, child_count, kv_heads):
    return jnp.transpose(stat.reshape(child_count, kv_heads, -1), (1, 0, 2))[..., None]


def local(
    child_parent,
    prefix_len,
    child_delta,
    parent_hidden,
    parent_cache,
    prefix_cache,
    norm_gain,
    w_query,
    w_kv,
):
    row_count = lax.axis_size("row")
    col_count = lax.axis_size("col")
    device_count = row_count * col_count
    my_row = lax.axis_index("row")
    my_col = lax.axis_index("col")
    my_device = my_row * col_count + my_col
    per_device = child_parent.shape[0]
    parent_count = parent_hidden.shape[0]
    whole_map = lax.all_gather(child_parent, ("row", "col"), axis=0, tiled=True)
    whole_source = whole_map // parent_count
    whole_local = whole_map % parent_count
    my_source = child_parent // parent_count
    capacity = 2 * ((per_device // (2 * col_count) + row_count - 1) // row_count)
    send_ids, flat_index = direct_layout(
        whole_source, whole_local, my_source, my_device, device_count, per_device, capacity
    )
    arrived_hidden = lax.all_to_all(
        parent_hidden[send_ids], ("row", "col"), split_axis=0, concat_axis=0, tiled=True
    )
    hidden_rows = arrived_hidden.reshape(-1, arrived_hidden.shape[-1])[flat_index]
    queries, new_kv = project_rows(hidden_rows, child_delta, norm_gain, w_query, w_kv)
    prefix_rows = prefix_cache[0]
    kv_heads = prefix_rows.shape[1]
    head_dim = prefix_rows.shape[-1]
    block_tokens = parent_cache.shape[3]
    scale_factor = 1.0 / math.sqrt(head_dim)
    grouped = queries.reshape(per_device, kv_heads, -1, head_dim)
    score_pre = prefix_scores(grouped, prefix_len, prefix_rows, block_tokens, scale_factor)
    top_pre = jnp.max(score_pre, axis=-1, keepdims=True)
    sum_pre = jnp.sum(jnp.exp(score_pre - top_pre), axis=-1, keepdims=True)
    slot_total = device_count * capacity
    query_box = jnp.zeros((slot_total, queries.shape[1]), jnp.bfloat16).at[flat_index].set(queries)
    top_box = (
        jnp.zeros((slot_total, queries.shape[1] // head_dim), jnp.float32)
        .at[flat_index]
        .set(heads_to_rows(top_pre, per_device))
    )
    sum_box = (
        jnp.zeros((slot_total, queries.shape[1] // head_dim), jnp.float32)
        .at[flat_index]
        .set(heads_to_rows(sum_pre, per_device))
    )
    far_query, far_top, far_sum = (
        lax.all_to_all(
            query_box.reshape(device_count, capacity, -1).astype(jnp.float32),
            ("row", "col"),
            split_axis=0,
            concat_axis=0,
            tiled=True,
        ).astype(jnp.bfloat16),
        lax.all_to_all(
            top_box.reshape(device_count, capacity, -1),
            ("row", "col"),
            split_axis=0,
            concat_axis=0,
            tiled=True,
        ),
        lax.all_to_all(
            sum_box.reshape(device_count, capacity, -1),
            ("row", "col"),
            split_axis=0,
            concat_axis=0,
            tiled=True,
        ),
    )
    own_blocks = parent_cache[send_ids.reshape(-1)]
    item_query = far_query.reshape(slot_total, kv_heads, -1, head_dim)
    score_par = (
        jnp.einsum(
            "chgd,chtd->hcgt", item_query, own_blocks[:, 0], preferred_element_type=jnp.float32
        )
        * scale_factor
    )
    remote_top = rows_to_heads(far_top, slot_total, kv_heads)
    remote_sum = rows_to_heads(far_sum, slot_total, kv_heads)
    joint_top = jnp.maximum(remote_top, jnp.max(score_par, axis=-1, keepdims=True))
    exp_par = jnp.exp(score_par - joint_top)
    joint_sum = remote_sum * jnp.exp(remote_top - joint_top) + jnp.sum(
        exp_par, axis=-1, keepdims=True
    )
    weight_par = (exp_par / joint_sum).astype(jnp.bfloat16)
    share = jnp.einsum(
        "hcgt,chtd->chgd", weight_par, own_blocks[:, 1], preferred_element_type=jnp.float32
    )
    back_share, back_top, back_sum = side_by_side(
        (
            share.reshape(device_count, capacity, -1),
            heads_to_rows(joint_top, slot_total).reshape(device_count, capacity, -1),
            heads_to_rows(joint_sum, slot_total).reshape(device_count, capacity, -1),
        ),
        ("row", "col"),
        0,
        0,
        2,
    )
    child_share = back_share.reshape(slot_total, -1)[flat_index]
    child_top = rows_to_heads(back_top.reshape(slot_total, -1)[flat_index], per_device, kv_heads)
    child_sum = rows_to_heads(back_sum.reshape(slot_total, -1)[flat_index], per_device, kv_heads)
    weight_pre = (jnp.exp(score_pre - child_top) / child_sum).astype(jnp.bfloat16)
    context = jnp.einsum(
        "hcgl,hld->chgd", weight_pre, prefix_rows[1], preferred_element_type=jnp.float32
    )
    context = context + child_share.reshape(context.shape)
    return (context.reshape(per_device, -1).astype(jnp.bfloat16), new_kv)


def solution(mesh):
    return jax.shard_map(
        local,
        mesh=mesh,
        in_specs=(
            P(("row", "col")),
            P(("row", "col")),
            P(("row", "col"), None),
            P(("row", "col"), None),
            P(("row", "col"), None, None, None, None),
            P(("row", "col"), None, None, None, None),
            P(),
            P(),
            P(),
        ),
        out_specs=(P(("row", "col"), None), P(("row", "col"), None)),
        check_vma=False,
    )
```

profile of v0, /device:TPU:1, one launch (start us, length us, event | category | flops | bytes accessed | tf_op | source)
XLA Modules:
  0.0 276.7 jit_solution(15527719592834599393)
XLA Ops:
  0.7 34.6 %all-gather = s32[128,1,128]{2,1,0:T(1,128)S(1)} all-gather(s32[1,1,128]{2,1,0:T(1,128)} %bitcast.107), channel_id=1, replica_groups=mesh['row'=16,'col'=8] {'row','col'}, dimensions={0}, use_global_device_ids=true | all-gather | bytes 66048 | tf_op jit(solution)/shard_map/all_gather | solution.py:84
  35.4 0.2 reduce_window_sum.11
  36.1 1.7 gather_fusion
  37.8 1.7 reshape.190
  39.5 7.2 %all-to-all-start = ((bf16[128,2,3584]{2,1,0:T(2,128)(2,1)}), bf16[128,2,3584]{2,1,0:T(2,128)(2,1)}, u32[]{:S(2)}, u32[]{:S(2)}) async-start(bf16[128,2,3584]{2,1,0:T(2,128)(2,1)} %reshape.190), calls=%async_computation | async-start | bytes 3670016 | tf_op jit(solution)/shard_map/all_to_all | solution.py:92
  46.9 0.4 iota_compare_fusion
  47.3 26.8 %all-to-all-done = bf16[128,2,3584]{2,1,0:T(2,128)(2,1)} async-done(((bf16[128,2,3584]{2,1,0:T(2,128)(2,1)}), bf16[128,2,3584]{2,1,0:T(2,128)(2,1)}, u32[]{:S(2)}, u32[]{:S(2)}) %all-to-all-start) | async-done | bytes 1835040 | tf_op jit(solution)/shard_map/all_to_all | solution.py:92
  74.1 4.1 %reshape.171 = bf16[256,3584]{1,0:T(8,128)(2,1)S(1)} reshape(bf16[128,2,3584]{2,1,0:T(2,128)(2,1)} %all-to-all-done) | data formatting | bytes 3670016 | tf_op jit(solution)/shard_map/reshape | solution.py:95
  78.2 2.0 gather_fusion.1
  80.2 1.8 multiply_reduce_fusion.1
  82.1 7.2 %convolution_convert_fusion = bf16[128,1792]{1,0:T(8,128)(2,1)S(1)} fusion(bf16[3584,1792]{1,0:T(8,128)(2,1)} %param.16, bf16[128,3584]{1,0:T(8,128)(2,1)} %param.11, bf16[128,3584]{1,0:T(8,128)(2,1)} %gather_fusion.1, f32[3584]{0:T(1024)S(1)} %copy-done.4, f32[128]{0:T(128)S(1)} %add_rsqrt_fusion), kind=kOutput, calls=%fused_computation.24 | convolution fusion | flops 1647149056 | bytes 15153664 | tf_op jit(solution)/shard_map/dot_general | solution.py:21
  89.3 0.3 copy.87
  89.5 16.7 %fusion = (f32[2,128,7]{1,2,0:T(8,128)S(1)}, f32[2,128,7,5120]{3,1,2,0:T(8,128)}) fusion(pred[128,5120]{1,0:T(8,128)(4,1)S(1)} %iota_compare_fusion, bf16[128,2,7,128]{0,3,2,1:T(8,128)(2,1)S(1)} %bitcast.95, bf16[1,2,2,5120,128]{4,3,2,1,0:T(8,128)(2,1)} %param.14), kind=kOutput, calls=%fused_computation.12 | convolution fusion | flops 2376333568 | bytes 40442880 | tf_op jit(solution)/shard_map/chgd,hld->hcgl/dot_general | solution.py:28
  106.3 1.5 scatter_custom_fusion.1
  107.8 4.3 %all-to-all-start.2 = ((f32[128,2,14]{2,1,0:T(2,128)}), f32[128,2,14]{2,1,0:T(2,128)S(1)}, u32[]{:S(2)}, u32[]{:S(2)}) async-start(f32[128,2,14]{2,1,0:T(2,128)} %bitcast.12), calls=%async_computation.2 | async-start | bytes 262144 | tf_op jit(solution)/shard_map/all_to_all | solution.py:126
  112.1 16.8 %exponential_reduce_fusion = f32[2,128,7]{1,2,0:T(8,128)S(1)} fusion(f32[2,128,7,5120]{3,1,2,0:T(8,128)} %get-tuple-element.21, f32[2,128,7]{1,2,0:T(8,128)S(1)} %get-tuple-element.20, pred[128,5120]{1,0:T(8,128)(4,1)S(1)} %iota_compare_fusion), kind=kLoop, calls=%fused_computation.10 | loop fusion | flops 36698368 | bytes 37369856 | tf_op jit(solution)/shard_map/reduce_sum | solution.py:105
  129.1 1.5 scatter_custom_fusion.2
  130.6 9.9 %all-to-all-start.3 = ((f32[128,2,14]{2,1,0:T(2,128)}), f32[128,2,14]{2,1,0:T(2,128)S(1)}, u32[]{:S(2)}, u32[]{:S(2)}) async-start(f32[128,2,14]{2,1,0:T(2,128)} %bitcast.15), calls=%async_computation.3 | async-start | bytes 262144 | tf_op jit(solution)/shard_map/all_to_all | solution.py:133
  140.5 1.6 scatter_custom_fusion
  142.1 1.3 reshape.188
  143.3 7.1 %all-to-all-done.3 = f32[128,2,14]{2,1,0:T(2,128)S(1)} async-done(((f32[128,2,14]{2,1,0:T(2,128)}), f32[128,2,14]{2,1,0:T(2,128)S(1)}, u32[]{:S(2)}, u32[]{:S(2)}) %all-to-all-start.3) | async-done | bytes 14368 | tf_op jit(solution)/shard_map/all_to_all | solution.py:133
  150.4 4.3 %all-to-all-start.1 = ((bf16[128,2,1792]{2,1,0:T(2,128)(2,1)}), bf16[128,2,1792]{2,1,0:T(2,128)(2,1)S(1)}, u32[]{:S(2)}, u32[]{:S(2)}) async-start(bf16[128,2,1792]{2,1,0:T(2,128)(2,1)} %reshape.188), calls=%async_computation.1 | async-start | bytes 1835008 | tf_op jit(solution)/shard_map/all_to_all | solution.py:119
  155.0 15.9 %gather_fusion.2 = bf16[256,2,2,128,128]{4,3,2,1,0:T(8,128)(2,1)} fusion(bf16[32,2,2,128,128]{4,3,2,1,0:T(8,128)(2,1)} %param.13, s32[1024]{0:T(1024)S(1)} %pad_clamp_fusion), kind=kCustom, calls=%fused_computation.2 | custom fusion | bytes 67109888 | tf_op jit(solution)/shard_map/gather | solution.py:141
  170.9 0.2 reshape.177
  171.2 0.3 reshape.180
  171.6 1.1 all-to-all-done.1
  172.7 1.6 reshape.173
  174.3 13.6 %multiply_reduce_fusion = (f32[2,256,7]{2,1,0:T(8,128)S(1)}, f32[2,256,7,128]{3,2,1,0:T(8,128)}) fusion(bf16[256,2,7,128]{3,2,1,0:T(8,128)(2,1)} %reshape.173, bf16[256,2,2,128,128]{4,3,2,1,0:T(8,128)(2,1)} %gather_fusion.2), kind=kOutput, calls=%fused_computation.27 | convolution fusion | flops 118354432 | bytes 19675136 | tf_op jit(solution)/shard_map/chgd,chtd->hcgt/dot_general | solution.py:144
  188.0 2.5 fusion.9
  190.7 9.8 %fusion.2 = f32[256,2,7,128]{3,2,1,0:T(8,128)} fusion(bf16[256,2,2,128,128]{4,3,2,1,0:T(8,128)(2,1)} %gather_fusion.2, f32[2,256,7,128]{3,2,1,0:T(8,128)} %get-tuple-element.19, f32[2,256,7]{2,1,0:T(8,128)S(1)} %fusion.23, f32[2,256,7]{2,1,0:T(8,128)S(1)} %bitcast_maximum_fusion), kind=kOutput, calls=%fused_computation.15 | convolution fusion | flops 119275520 | bytes 20738048 | tf_op jit(solution)/shard_map/hcgt,chtd->chgd/dot_general | solution.py:157
  200.5 2.3 reshape.181
  202.8 0.2 copy.104
  203.0 0.3 reshape_reshape.7
  203.3 0.2 copy.100
  203.5 0.3 reshape_reshape.6
  203.7 4.2 %concatenate.3 = f32[128,2,1820]{2,1,0:T(2,128)} concatenate(f32[128,2,1792]{2,1,0:T(2,128)S(1)} %reshape.181, f32[128,2,14]{2,1,0:T(2,128)S(1)} %reshape_reshape.6, f32[128,2,14]{2,1,0:T(2,128)S(1)} %reshape_reshape.7), dimensions={2} | concatenate | bytes 3727360 | tf_op jit(solution)/shard_map/concatenate | solution.py:12
  207.9 9.1 %all-to-all-start.4 = ((f32[128,2,1820]{2,1,0:T(2,128)}), f32[128,2,1820]{2,1,0:T(2,128)}, u32[]{:S(2)}, u32[]{:S(2)}) async-start(f32[128,2,1820]{2,1,0:T(2,128)} %concatenate.3), calls=%async_computation.4 | async-start | bytes 3932160 | tf_op jit(solution)/shard_map/all_to_all | solution.py:13
  217.1 3.4 %convolution_convert_fusion.1 = bf16[128,512]{1,0:T(8,128)(2,1)} fusion(bf16[3584,512]{1,0:T(8,128)(2,1)} %param.17, bf16[128,3584]{1,0:T(8,128)(2,1)S(1)} %copy-done.3, bf16[128,3584]{1,0:T(8,128)(2,1)S(1)} %copy-done.2, f32[3584]{0:T(1024)S(1)} %copy-done.4, f32[128]{0:T(128)S(1)} %add_rsqrt_fusion), kind=kOutput, calls=%fused_computation.35 | convolution fusion | flops 472580096 | bytes 5650944 | tf_op jit(solution)/shard_map/dot_general | solution.py:22
  220.5 25.5 %all-to-all-done.4 = f32[128,2,1820]{2,1,0:T(2,128)} async-done(((f32[128,2,1820]{2,1,0:T(2,128)}), f32[128,2,1820]{2,1,0:T(2,128)}, u32[]{:S(2)}, u32[]{:S(2)}) %all-to-all-start.4) | async-done | bytes 1863712 | tf_op jit(solution)/shard_map/all_to_all | solution.py:13
  245.9 2.9 %split.14 = f32[128,2,1792]{2,1,0:T(2,128)} slice(f32[128,2,1820]{2,1,0:T(2,128)} %all-to-all-done.4), slice={[0:128], [0:2], [0:1792]} | slice | bytes 3670016 | tf_op jit(solution)/shard_map/split | solution.py:14
  248.8 2.5 reshape.186
  251.4 1.9 gather_fusion.5
  253.2 1.5 copy.108
  254.7 1.2 fusion.40
  255.9 0.6 gather_fusion.3
  256.6 0.7 gather_fusion.4
  257.4 18.4 %fusion.16 = bf16[128,2,7,128]{0,3,2,1:T(8,128)(2,1)S(1)} fusion(f32[128,2,7,128]{0,3,2,1:T(8,128)S(1)} %bitcast.98, bf16[1,2,2,5120,128]{4,3,2,1,0:T(8,128)(2,1)} %param.14, f32[2,128,7,5120]{3,1,2,0:T(8,128)} %get-tuple-element.21, f32[2,128,7]{1,2,0:T(8,128)S(1)} %bitcast.105, f32[2,128,7]{1,2,0:T(8,128)S(1)} %bitcast.104, ...), kind=kOutput, calls=%fused_computation.34 | convolution fusion | flops 2395144192 | bytes 41367552 | tf_op jit(solution)/shard_map/hcgl,hld->chgd/dot_general | solution.py:175
  275.7 1.0 copy.109
  (50 shorter events, 2.1 us)
Async XLA Ops:
  0.6 35.5 %copy-start = (bf16[32,3584]{1,0:T(8,128)(2,1)S(1)}, bf16[32,3584]{1,0:T(8,128)(2,1)}, u32[]{:S(2)}) copy-start(bf16[32,3584]{1,0:T(8,128)(2,1)} %param.12) | copy-start | bytes 688132
  39.5 7.2 %copy-start.5 = (s32[128]{0:T(128)S(1)}, s32[128]{0:T(128)}, u32[]{:S(2)}) copy-start(s32[128]{0:T(128)} %param.9) | copy-start | bytes 1540
  39.5 7.4 %copy-start.6 = (s32[128]{0:T(128)S(1)}, s32[128]{0:T(128)}, u32[]{:S(2)}) copy-start(s32[128]{0:T(128)} %param.10) | copy-start | bytes 1540
  39.5 34.6 %all-to-all-start = ((bf16[128,2,3584]{2,1,0:T(2,128)(2,1)}), bf16[128,2,3584]{2,1,0:T(2,128)(2,1)}, u32[]{:S(2)}, u32[]{:S(2)}) async-start(bf16[128,2,3584]{2,1,0:T(2,128)(2,1)} %reshape.190), calls=%async_computation | async-start | bytes 3670016 | tf_op jit(solution)/shard_map/all_to_all | solution.py:92
  78.2 3.9 %copy-start.4 = (f32[3584]{0:T(1024)S(1)}, f32[3584]{0:T(1024)}, u32[]{:S(2)}) copy-start(f32[3584]{0:T(1024)} %param.15) | copy-start | bytes 43012
  107.8 22.7 %all-to-all-start.2 = ((f32[128,2,14]{2,1,0:T(2,128)}), f32[128,2,14]{2,1,0:T(2,128)S(1)}, u32[]{:S(2)}, u32[]{:S(2)}) async-start(f32[128,2,14]{2,1,0:T(2,128)} %bitcast.12), calls=%async_computation.2 | async-start | bytes 262144 | tf_op jit(solution)/shard_map/all_to_all | solution.py:126
  130.6 19.9 %all-to-all-start.3 = ((f32[128,2,14]{2,1,0:T(2,128)}), f32[128,2,14]{2,1,0:T(2,128)S(1)}, u32[]{:S(2)}, u32[]{:S(2)}) async-start(f32[128,2,14]{2,1,0:T(2,128)} %bitcast.15), calls=%async_computation.3 | async-start | bytes 262144 | tf_op jit(solution)/shard_map/all_to_all | solution.py:133
  150.4 22.2 %all-to-all-start.1 = ((bf16[128,2,1792]{2,1,0:T(2,128)(2,1)}), bf16[128,2,1792]{2,1,0:T(2,128)(2,1)S(1)}, u32[]{:S(2)}, u32[]{:S(2)}) async-start(bf16[128,2,1792]{2,1,0:T(2,128)(2,1)} %reshape.188), calls=%async_computation.1 | async-start | bytes 1835008 | tf_op jit(solution)/shard_map/all_to_all | solution.py:119
  207.9 9.1 %copy-start.2 = (bf16[128,3584]{1,0:T(8,128)(2,1)S(1)}, bf16[128,3584]{1,0:T(8,128)(2,1)}, u32[]{:S(2)}) copy-start(bf16[128,3584]{1,0:T(8,128)(2,1)} %gather_fusion.1) | copy-start | bytes 2752516
  207.9 9.1 %copy-start.3 = (bf16[128,3584]{1,0:T(8,128)(2,1)S(1)}, bf16[128,3584]{1,0:T(8,128)(2,1)}, u32[]{:S(2)}) copy-start(bf16[128,3584]{1,0:T(8,128)(2,1)} %param.11) | copy-start | bytes 2752516
  207.9 38.0 %all-to-all-start.4 = ((f32[128,2,1820]{2,1,0:T(2,128)}), f32[128,2,1820]{2,1,0:T(2,128)}, u32[]{:S(2)}, u32[]{:S(2)}) async-start(f32[128,2,1820]{2,1,0:T(2,128)} %concatenate.3), calls=%async_computation.4 | async-start | bytes 3932160 | tf_op jit(solution)/shard_map/all_to_all | solution.py:13
  257.4 19.4 %copy-start.1 = (bf16[32,3584]{1,0:T(8,128)(2,1)S(1)}, bf16[32,3584]{1,0:T(8,128)(2,1)}, u32[]{:S(2)}) copy-start(bf16[32,3584]{1,0:T(8,128)(2,1)} %param.12) | copy-start | bytes 688132
where the time goes:
time: 278 us; the launch traced here: 277 us
  matrix products  69 us (25%)
  waiting for transfers between devices  60.4 us (22%)
  local copies, waits for them, and re-layouts  54.7 us (20%)
  starting transfers between devices  34.7 us (12%)
  blocking collectives  34.6 us (12%)
  other arithmetic  22.3 us (8%)
    all_gather x1, blocking collectives, local(): whole_map = lax.all_gather(child_parent, ('row', 'col'), axis=0, tiled=True)  34.6 us
    all_to_all x1, waiting for transfers between devices, local(): lax.all_to_all(parent_hidden[send_ids], ('row', 'col'), split_axis=0, con...  26.8 us
    all_to_all x1, waiting for transfers between devices, side_by_side(): lax.all_to_all(both, axis, split_axis=split_dim, concat_axis=concat_dim,...  25.5 us
    dot_general x1, matrix products, local(): jnp.einsum('hcgl,hld->chgd', weight_pre, prefix_rows[1], preferred_elemen...  18.4 us
    reduce_sum x1, other arithmetic, local(): sum_pre = jnp.sum(jnp.exp(score_pre - top_pre), axis=-1, keepdims=True)  16.8 us
    dot_general x1, matrix products, prefix_scores(): jnp.einsum('chgd,hld->hcgl', grouped, prefix_rows[0], preferred_element_t...  16.7 us
    gather x1, local copies, waits for them, and re-layouts, local(): own_blocks = parent_cache[send_ids.reshape(-1)]  15.9 us
    dot_general x1, matrix products, local(): jnp.einsum('chgd,chtd->hcgt', item_query, own_blocks[:, 0], preferred_ele...  13.6 us
  transfers between devices with their start and end apart: 5, of which 4 were waited for; matrix products, arithmetic and copies ran while one was open for 15% of the time, Pallas kernels for 0%

commit v1 on v0

--- a/solution.py
+++ b/solution.py
@@ -81,7 +81,12 @@
     my_device = my_row * col_count + my_col
     per_device = child_parent.shape[0]
     parent_count = parent_hidden.shape[0]
-    whole_map = lax.all_gather(child_parent, ("row", "col"), axis=0, tiled=True)
+    whole_map = jnp.concatenate(
+        lax.all_to_all(
+            jnp.stack([child_parent] * lax.axis_size(("row", "col"))), ("row", "col"), 0, 0
+        ),
+        axis=0,
+    )
     whole_source = whole_map // parent_count
     whole_local = whole_map % parent_count
     my_source = child_parent // parent_count

time: 278 us -> 264 us (0.950)
  blocking collectives: 34.6 us -> 0 us
  starting transfers between devices: 34.7 us -> 44.5 us
  waiting for transfers between devices: 60.4 us -> 70 us
    all_gather x1 -> x0, blocking collectives: 34.6 us -> none  [local(): whole_map = lax.all_gather(child_parent, ('row', 'col'), axis=0, tiled=True)]
    all_to_all x0 -> x1, starting transfers between devices: none -> 11.5 us  [local(): lax.all_to_all(jnp.stack([child_parent] * lax.axis_size(('row', 'col'))),...]
    all_to_all x0 -> x1, waiting for transfers between devices: none -> 9.41 us  [local(): lax.all_to_all(jnp.stack([child_parent] * lax.axis_size(('row', 'col'))),...]
  transfers between devices with their start and end apart: 5 -> 6, of which waited for: 4 -> 5; matrix products, arithmetic and copies ran while one was open for 15% -> 16% of each run, Pallas kernels for 0% -> 0%
where the time goes in v1:
time: 264 us; the launch traced here: 263 us
  waiting for transfers between devices  70 us (27%)
  matrix products  69 us (26%)
  local copies, waits for them, and re-layouts  56.1 us (21%)
  starting transfers between devices  44.5 us (17%)
  other arithmetic  22.3 us (8%)
    all_to_all x1, waiting for transfers between devices, local(): lax.all_to_all(parent_hidden[send_ids], ('row', 'col'), split_axis=0, con...  26.9 us
    all_to_all x1, waiting for transfers between devices, side_by_side(): lax.all_to_all(both, axis, split_axis=split_dim, concat_axis=concat_dim,...  25.5 us
    dot_general x1, matrix products, local(): jnp.einsum('hcgl,hld->chgd', weight_pre, prefix_rows[1], preferred_elemen...  18.4 us
    reduce_sum x1, other arithmetic, local(): sum_pre = jnp.sum(jnp.exp(score_pre - top_pre), axis=-1, keepdims=True)  16.8 us
    dot_general x1, matrix products, prefix_scores(): jnp.einsum('chgd,hld->hcgl', grouped, prefix_rows[0], preferred_element_t...  16.7 us
    gather x1, local copies, waits for them, and re-layouts, local(): own_blocks = parent_cache[send_ids.reshape(-1)]  15.9 us
    dot_general x1, matrix products, local(): jnp.einsum('chgd,chtd->hcgt', item_query, own_blocks[:, 0], preferred_ele...  13.6 us
    all_to_all x1, starting transfers between devices, local(): lax.all_to_all(jnp.stack([child_parent] * lax.axis_size(('row', 'col'))),...  11.5 us
  transfers between devices with their start and end apart: 6, of which 5 were waited for; matrix products, arithmetic and copies ran while one was open for 16% of the time, Pallas kernels for 0%

profile of v1, /device:TPU:1, one launch (start us, length us, event | category | flops | bytes accessed | tf_op | source)
XLA Modules:
  0.0 262.9 jit_solution(12295529589535874915)
XLA Ops:
  0.6 1.4 stack.2
  2.0 11.5 %all-to-all-start = ((s32[128,1,128]{2,1,0:T(1,128)}), s32[128,1,128]{2,1,0:T(1,128)S(1)}, u32[]{:S(2)}, u32[]{:S(2)}) async-start(s32[128,1,128]{2,1,0:T(1,128)} %stack.2), calls=%async_computation | async-start | bytes 131072 | tf_op jit(solution)/shard_map/all_to_all | solution.py:85
  13.5 9.4 %all-to-all-done = s32[128,1,128]{2,1,0:T(1,128)S(1)} async-done(((s32[128,1,128]{2,1,0:T(1,128)}), s32[128,1,128]{2,1,0:T(1,128)S(1)}, u32[]{:S(2)}, u32[]{:S(2)}) %all-to-all-start) | async-done | bytes 65568 | tf_op jit(solution)/shard_map/all_to_all | solution.py:85
  23.8 1.7 gather_fusion
  25.5 1.7 reshape.187
  27.2 5.4 %all-to-all-start.1 = ((bf16[128,2,3584]{2,1,0:T(2,128)(2,1)}), bf16[128,2,3584]{2,1,0:T(2,128)(2,1)}, u32[]{:S(2)}, u32[]{:S(2)}) async-start(bf16[128,2,3584]{2,1,0:T(2,128)(2,1)} %reshape.187), calls=%async_computation.1 | async-start | bytes 3670016 | tf_op jit(solution)/shard_map/all_to_all | solution.py:97
  32.9 0.4 iota_compare_fusion
  33.3 26.9 %all-to-all-done.1 = bf16[128,2,3584]{2,1,0:T(2,128)(2,1)} async-done(((bf16[128,2,3584]{2,1,0:T(2,128)(2,1)}), bf16[128,2,3584]{2,1,0:T(2,128)(2,1)}, u32[]{:S(2)}, u32[]{:S(2)}) %all-to-all-start.1) | async-done | bytes 1835040 | tf_op jit(solution)/shard_map/all_to_all | solution.py:97
  60.3 4.1 %reshape.168 = bf16[256,3584]{1,0:T(8,128)(2,1)S(1)} reshape(bf16[128,2,3584]{2,1,0:T(2,128)(2,1)} %all-to-all-done.1) | data formatting | bytes 3670016 | tf_op jit(solution)/shard_map/reshape | solution.py:100
  64.3 2.0 gather_fusion.1
  66.4 1.8 multiply_reduce_fusion.1
  68.2 7.2 %convolution_convert_fusion = bf16[128,1792]{1,0:T(8,128)(2,1)S(1)} fusion(bf16[3584,1792]{1,0:T(8,128)(2,1)} %param.16, bf16[128,3584]{1,0:T(8,128)(2,1)} %param.11, bf16[128,3584]{1,0:T(8,128)(2,1)} %gather_fusion.1, f32[3584]{0:T(1024)S(1)} %copy-done.4, f32[128]{0:T(128)S(1)} %add_rsqrt_fusion), kind=kOutput, calls=%fused_computation.24 | convolution fusion | flops 1647149056 | bytes 15153664 | tf_op jit(solution)/shard_map/dot_general | solution.py:21
  75.4 0.3 copy.123
  75.7 16.7 %fusion = (f32[2,128,7]{1,2,0:T(8,128)S(1)}, f32[2,128,7,5120]{3,1,2,0:T(8,128)}) fusion(pred[128,5120]{1,0:T(8,128)(4,1)S(1)} %iota_compare_fusion, bf16[128,2,7,128]{0,3,2,1:T(8,128)(2,1)S(1)} %bitcast.97, bf16[1,2,2,5120,128]{4,3,2,1,0:T(8,128)(2,1)} %param.14), kind=kOutput, calls=%fused_computation.12 | convolution fusion | flops 2376333568 | bytes 40442880 | tf_op jit(solution)/shard_map/chgd,hld->hcgl/dot_general | solution.py:28
  92.5 1.5 scatter_custom_fusion.1
  94.0 4.3 %all-to-all-start.3 = ((f32[128,2,14]{2,1,0:T(2,128)}), f32[128,2,14]{2,1,0:T(2,128)S(1)}, u32[]{:S(2)}, u32[]{:S(2)}) async-start(f32[128,2,14]{2,1,0:T(2,128)} %bitcast.14), calls=%async_computation.3 | async-start | bytes 262144 | tf_op jit(solution)/shard_map/all_to_all | solution.py:131
  98.3 16.8 %exponential_reduce_fusion = f32[2,128,7]{1,2,0:T(8,128)S(1)} fusion(f32[2,128,7,5120]{3,1,2,0:T(8,128)} %get-tuple-element.23, f32[2,128,7]{1,2,0:T(8,128)S(1)} %get-tuple-element.22, pred[128,5120]{1,0:T(8,128)(4,1)S(1)} %iota_compare_fusion), kind=kLoop, calls=%fused_computation.10 | loop fusion | flops 36698368 | bytes 37369856 | tf_op jit(solution)/shard_map/reduce_sum | solution.py:110
  115.2 1.5 scatter_custom_fusion.2
  116.7 9.9 %all-to-all-start.4 = ((f32[128,2,14]{2,1,0:T(2,128)}), f32[128,2,14]{2,1,0:T(2,128)S(1)}, u32[]{:S(2)}, u32[]{:S(2)}) async-start(f32[128,2,14]{2,1,0:T(2,128)} %bitcast.17), calls=%async_computation.4 | async-start | bytes 262144 | tf_op jit(solution)/shard_map/all_to_all | solution.py:138
  126.6 1.6 scatter_custom_fusion
  128.2 1.3 reshape.185
  129.5 7.1 %all-to-all-done.4 = f32[128,2,14]{2,1,0:T(2,128)S(1)} async-done(((f32[128,2,14]{2,1,0:T(2,128)}), f32[128,2,14]{2,1,0:T(2,128)S(1)}, u32[]{:S(2)}, u32[]{:S(2)}) %all-to-all-start.4) | async-done | bytes 14368 | tf_op jit(solution)/shard_map/all_to_all | solution.py:138
  136.6 4.3 %all-to-all-start.2 = ((bf16[128,2,1792]{2,1,0:T(2,128)(2,1)}), bf16[128,2,1792]{2,1,0:T(2,128)(2,1)S(1)}, u32[]{:S(2)}, u32[]{:S(2)}) async-start(bf16[128,2,1792]{2,1,0:T(2,128)(2,1)} %reshape.185), calls=%async_computation.2 | async-start | bytes 1835008 | tf_op jit(solution)/shard_map/all_to_all | solution.py:124
  141.2 15.9 %gather_fusion.2 = bf16[256,2,2,128,128]{4,3,2,1,0:T(8,128)(2,1)} fusion(bf16[32,2,2,128,128]{4,3,2,1,0:T(8,128)(2,1)} %param.13, s32[1024]{0:T(1024)S(1)} %pad_clamp_fusion), kind=kCustom, calls=%fused_computation.2 | custom fusion | bytes 67109888 | tf_op jit(solution)/shard_map/gather | solution.py:146
  157.0 0.2 reshape.174
  157.4 0.3 reshape.177
  157.7 1.1 all-to-all-done.2
  158.8 1.6 reshape.170
  160.4 13.6 %multiply_reduce_fusion = (f32[2,256,7]{2,1,0:T(8,128)S(1)}, f32[2,256,7,128]{3,2,1,0:T(8,128)}) fusion(bf16[256,2,7,128]{3,2,1,0:T(8,128)(2,1)} %reshape.170, bf16[256,2,2,128,128]{4,3,2,1,0:T(8,128)(2,1)} %gather_fusion.2), kind=kOutput, calls=%fused_computation.27 | convolution fusion | flops 118354432 | bytes 19675136 | tf_op jit(solution)/shard_map/chgd,chtd->hcgt/dot_general | solution.py:149
  174.1 2.5 fusion.9
  176.9 9.8 %fusion.2 = f32[256,2,7,128]{3,2,1,0:T(8,128)} fusion(bf16[256,2,2,128,128]{4,3,2,1,0:T(8,128)(2,1)} %gather_fusion.2, f32[2,256,7,128]{3,2,1,0:T(8,128)} %get-tuple-element.21, f32[2,256,7]{2,1,0:T(8,128)S(1)} %fusion.23, f32[2,256,7]{2,1,0:T(8,128)S(1)} %bitcast_maximum_fusion), kind=kOutput, calls=%fused_computation.15 | convolution fusion | flops 119275520 | bytes 20738048 | tf_op jit(solution)/shard_map/hcgt,chtd->chgd/dot_general | solution.py:162
  186.6 2.3 reshape.178
  189.0 0.2 copy.140
  189.2 0.3 reshape_reshape.7
  189.6 0.3 reshape_reshape.6
  189.9 4.2 %concatenate.3 = f32[128,2,1820]{2,1,0:T(2,128)} concatenate(f32[128,2,1792]{2,1,0:T(2,128)S(1)} %reshape.178, f32[128,2,14]{2,1,0:T(2,128)S(1)} %reshape_reshape.6, f32[128,2,14]{2,1,0:T(2,128)S(1)} %reshape_reshape.7), dimensions={2} | concatenate | bytes 3727360 | tf_op jit(solution)/shard_map/concatenate | solution.py:12
  194.1 9.1 %all-to-all-start.5 = ((f32[128,2,1820]{2,1,0:T(2,128)}), f32[128,2,1820]{2,1,0:T(2,128)}, u32[]{:S(2)}, u32[]{:S(2)}) async-start(f32[128,2,1820]{2,1,0:T(2,128)} %concatenate.3), calls=%async_computation.5 | async-start | bytes 3932160 | tf_op jit(solution)/shard_map/all_to_all | solution.py:13
  203.2 3.4 %convolution_convert_fusion.1 = bf16[128,512]{1,0:T(8,128)(2,1)} fusion(bf16[3584,512]{1,0:T(8,128)(2,1)} %param.17, bf16[128,3584]{1,0:T(8,128)(2,1)S(1)} %copy-done.3, bf16[128,3584]{1,0:T(8,128)(2,1)S(1)} %copy-done.2, f32[3584]{0:T(1024)S(1)} %copy-done.4, f32[128]{0:T(128)S(1)} %add_rsqrt_fusion), kind=kOutput, calls=%fused_computation.35 | convolution fusion | flops 472580096 | bytes 5650944 | tf_op jit(solution)/shard_map/dot_general | solution.py:22
  206.6 25.5 %all-to-all-done.5 = f32[128,2,1820]{2,1,0:T(2,128)} async-done(((f32[128,2,1820]{2,1,0:T(2,128)}), f32[128,2,1820]{2,1,0:T(2,128)}, u32[]{:S(2)}, u32[]{:S(2)}) %all-to-all-start.5) | async-done | bytes 1863712 | tf_op jit(solution)/shard_map/all_to_all | solution.py:13
  232.1 2.9 %split.14 = f32[128,2,1792]{2,1,0:T(2,128)} slice(f32[128,2,1820]{2,1,0:T(2,128)} %all-to-all-done.5), slice={[0:128], [0:2], [0:1792]} | slice | bytes 3670016 | tf_op jit(solution)/shard_map/split | solution.py:14
  234.9 2.5 reshape.183
  237.5 1.9 gather_fusion.5
  239.4 1.5 copy.144
  240.9 1.2 fusion.40
  242.0 0.6 gather_fusion.3
  242.8 0.7 gather_fusion.4
  243.5 18.4 %fusion.16 = bf16[128,2,7,128]{0,3,2,1:T(8,128)(2,1)S(1)} fusion(f32[128,2,7,128]{0,3,2,1:T(8,128)S(1)} %bitcast.100, bf16[1,2,2,5120,128]{4,3,2,1,0:T(8,128)(2,1)} %param.14, f32[2,128,7,5120]{3,1,2,0:T(8,128)} %get-tuple-element.23, f32[2,128,7]{1,2,0:T(8,128)S(1)} %bitcast.107, f32[2,128,7]{1,2,0:T(8,128)S(1)} %bitcast.106, ...), kind=kOutput, calls=%fused_computation.34 | convolution fusion | flops 2395144192 | bytes 41367552 | tf_op jit(solution)/shard_map/hcgl,hld->chgd/dot_general | solution.py:180
  261.9 1.0 copy.145
  (52 shorter events, 2.4 us)
Async XLA Ops:
  0.6 23.2 %copy-start = (bf16[32,3584]{1,0:T(8,128)(2,1)S(1)}, bf16[32,3584]{1,0:T(8,128)(2,1)}, u32[]{:S(2)}) copy-start(bf16[32,3584]{1,0:T(8,128)(2,1)} %param.12) | copy-start | bytes 688132
  2.0 20.9 %all-to-all-start = ((s32[128,1,128]{2,1,0:T(1,128)}), s32[128,1,128]{2,1,0:T(1,128)S(1)}, u32[]{:S(2)}, u32[]{:S(2)}) async-start(s32[128,1,128]{2,1,0:T(1,128)} %stack.2), calls=%async_computation | async-start | bytes 131072 | tf_op jit(solution)/shard_map/all_to_all | solution.py:85
  27.2 5.5 %copy-start.5 = (s32[128]{0:T(128)S(1)}, s32[128]{0:T(128)}, u32[]{:S(2)}) copy-start(s32[128]{0:T(128)} %param.9) | copy-start | bytes 1540
  27.2 5.7 %copy-start.6 = (s32[128]{0:T(128)S(1)}, s32[128]{0:T(128)}, u32[]{:S(2)}) copy-start(s32[128]{0:T(128)} %param.10) | copy-start | bytes 1540
  27.2 33.1 %all-to-all-start.1 = ((bf16[128,2,3584]{2,1,0:T(2,128)(2,1)}), bf16[128,2,3584]{2,1,0:T(2,128)(2,1)}, u32[]{:S(2)}, u32[]{:S(2)}) async-start(bf16[128,2,3584]{2,1,0:T(2,128)(2,1)} %reshape.187), calls=%async_computation.1 | async-start | bytes 3670016 | tf_op jit(solution)/shard_map/all_to_all | solution.py:97
  64.3 3.9 %copy-start.4 = (f32[3584]{0:T(1024)S(1)}, f32[3584]{0:T(1024)}, u32[]{:S(2)}) copy-start(f32[3584]{0:T(1024)} %param.15) | copy-start | bytes 43012
  94.0 22.7 %all-to-all-start.3 = ((f32[128,2,14]{2,1,0:T(2,128)}), f32[128,2,14]{2,1,0:T(2,128)S(1)}, u32[]{:S(2)}, u32[]{:S(2)}) async-start(f32[128,2,14]{2,1,0:T(2,128)} %bitcast.14), calls=%async_computation.3 | async-start | bytes 262144 | tf_op jit(solution)/shard_map/all_to_all | solution.py:131
  116.7 19.9 %all-to-all-start.4 = ((f32[128,2,14]{2,1,0:T(2,128)}), f32[128,2,14]{2,1,0:T(2,128)S(1)}, u32[]{:S(2)}, u32[]{:S(2)}) async-start(f32[128,2,14]{2,1,0:T(2,128)} %bitcast.17), calls=%async_computation.4 | async-start | bytes 262144 | tf_op jit(solution)/shard_map/all_to_all | solution.py:138
  136.6 22.2 %all-to-all-start.2 = ((bf16[128,2,1792]{2,1,0:T(2,128)(2,1)}), bf16[128,2,1792]{2,1,0:T(2,128)(2,1)S(1)}, u32[]{:S(2)}, u32[]{:S(2)}) async-start(bf16[128,2,1792]{2,1,0:T(2,128)(2,1)} %reshape.185), calls=%async_computation.2 | async-start | bytes 1835008 | tf_op jit(solution)/shard_map/all_to_all | solution.py:124
  194.1 9.1 %copy-start.2 = (bf16[128,3584]{1,0:T(8,128)(2,1)S(1)}, bf16[128,3584]{1,0:T(8,128)(2,1)}, u32[]{:S(2)}) copy-start(bf16[128,3584]{1,0:T(8,128)(2,1)} %gather_fusion.1) | copy-start | bytes 2752516
  194.1 9.1 %copy-start.3 = (bf16[128,3584]{1,0:T(8,128)(2,1)S(1)}, bf16[128,3584]{1,0:T(8,128)(2,1)}, u32[]{:S(2)}) copy-start(bf16[128,3584]{1,0:T(8,128)(2,1)} %param.11) | copy-start | bytes 2752516
  194.1 38.0 %all-to-all-start.5 = ((f32[128,2,1820]{2,1,0:T(2,128)}), f32[128,2,1820]{2,1,0:T(2,128)}, u32[]{:S(2)}, u32[]{:S(2)}) async-start(f32[128,2,1820]{2,1,0:T(2,128)} %concatenate.3), calls=%async_computation.5 | async-start | bytes 3932160 | tf_op jit(solution)/shard_map/all_to_all | solution.py:13
  243.5 19.4 %copy-start.1 = (bf16[32,3584]{1,0:T(8,128)(2,1)S(1)}, bf16[32,3584]{1,0:T(8,128)(2,1)}, u32[]{:S(2)}) copy-start(bf16[32,3584]{1,0:T(8,128)(2,1)} %param.12) | copy-start | bytes 688132
